TPU v7x, 512 devices: a whole 4x8x8 slice. The times are simulated.
512 devices in a mesh: ctx: 128 (over y, x_hi, z), head: 4 (over x_lo, core).
Axes of the slice: x: 4 (x_hi: 2, x_lo: 2; x = x_hi * 2 + x_lo), y: 8, z: 8, core: 2. Of those that a mesh axis runs over, the one named last changes fastest.
Arguments:
- text_query: bfloat16 [16384, 2560], P('ctx', 'head')
- grad_out: bfloat16 [16384, 2560], P('ctx', 'head'), may hold values from -6 to 6
- frame_kv: bfloat16 [2, 65536, 2560], P(None, 'ctx', 'head')
- sink_logit: float32 [20], P('head'), may hold values from 1 to 6
- pairing: int32 [128], replicated, may hold values from 0 to 127, each once
- block_mask: int32 [128, 4], P('ctx'), may hold values from 0 to 1
- text_seg: int32 [16384], P('ctx'), may hold values from 0 to 3, as said below
- frame_seg: int32 [65536], P('ctx'), may hold values from 0 to 3, as said below
Outputs:
- grad_query: bfloat16 [16384, 2560], P('ctx', 'head')
- grad_kv: bfloat16 [2, 65536, 2560], P(None, ('ctx', 'head'))
Inputs may be any that keep to these rules, and one draw needn't show every extreme that they name: pairing is a permutation of the ctx indices. `text_seg`: within the 128 text tokens of each ctx index the ids do not fall and each of the 4 ids appears. `frame_seg`: within the 512 frames of each ctx index the ids do not fall and each of the 4 ids appears.
All inputs are finite; a program needn't handle non-finite values.
Results may differ from a plain program's by a relative error of at most 0.0081.
Values may be sent and summed in bfloat16 or wider, within the bound.
A program may use at most 64 MiB of HBM per device.

v0:
```python
import jax
import jax.numpy as jnp
from jax import lax
from jax.sharding import PartitionSpec as P

DH = 128
BLOCK = 128


def attend(query_rows, grad_rows, key_rows, value_rows, row_mask, text_ids, frame_ids, sink_logit):
    score_scale = DH ** (-0.5)
    text_rows = query_rows.shape[0]
    frame_rows = key_rows.shape[0]
    head_count = query_rows.shape[1] // DH
    q_heads = query_rows.reshape(text_rows, head_count, DH)
    g_heads = grad_rows.reshape(text_rows, head_count, DH)
    k_heads = key_rows.reshape(frame_rows, head_count, DH)
    v_heads = value_rows.reshape(frame_rows, head_count, DH)
    allowed = (jnp.repeat(row_mask, BLOCK, axis=1) == 1) & (text_ids[:, None] == frame_ids[None, :])
    scores = (
        jnp.einsum("the,fhe->htf", q_heads, k_heads, preferred_element_type=jnp.float32)
        * score_scale
    )
    masked = jnp.where(allowed[None], scores, -1e30)
    row_top = jnp.maximum(sink_logit[:, None], jnp.max(masked, axis=2))
    exp_terms = jnp.where(allowed[None], jnp.exp(masked - row_top[:, :, None]), 0.0)
    row_total = jnp.exp(sink_logit[:, None] - row_top) + jnp.sum(exp_terms, axis=2)
    attention = exp_terms / row_total[:, :, None]
    attention_low = attention.astype(jnp.bfloat16)
    output = jnp.einsum("htf,fhe->the", attention_low, v_heads, preferred_element_type=jnp.float32)
    grad_attention = jnp.einsum(
        "the,fhe->htf", g_heads, v_heads, preferred_element_type=jnp.float32
    )
    row_delta = jnp.sum(g_heads.astype(jnp.float32) * output, axis=2)
    grad_scores = (attention * (grad_attention - row_delta.T[:, :, None])).astype(jnp.bfloat16)
    grad_query = (
        jnp.einsum("htf,fhe->the", grad_scores, k_heads, preferred_element_type=jnp.float32)
        * score_scale
    )
    grad_keys = (
        jnp.einsum("htf,the->fhe", grad_scores, q_heads, preferred_element_type=jnp.float32)
        * score_scale
    )
    grad_values = jnp.einsum(
        "htf,the->fhe", attention_low, g_heads, preferred_element_type=jnp.float32
    )
    grad_pair = jnp.stack([grad_keys.reshape(frame_rows, -1), grad_values.reshape(frame_rows, -1)])
    return (grad_query.reshape(text_rows, -1).astype(jnp.bfloat16), grad_pair.astype(jnp.bfloat16))


def shards(text_query, grad_out, frame_kv, sink_logit, pairing, block_mask, text_seg, frame_seg):
    owners = lax.axis_size("ctx")
    text_rows = text_query.shape[0]
    feature_width = text_query.shape[1]
    frame_blocks = block_mask.shape[1]
    indices = jnp.arange(owners, dtype=jnp.int32)
    inverse = jnp.sum(jnp.where(pairing[None, :] == indices[:, None], indices[None, :], 0), axis=1)
    row_mask = jnp.repeat(block_mask, BLOCK, axis=0)
    stacked = jnp.stack([text_query, grad_out]).reshape(
        2, owners, text_rows // owners, feature_width
    )
    text_tags = jnp.concatenate([text_seg[:, None], row_mask], axis=1).astype(jnp.bfloat16)
    text_tags = text_tags.reshape(1, owners, text_rows // owners, frame_blocks + 1)
    first_text, first_tags = (
        lax.all_to_all(stacked, "ctx", split_axis=1, concat_axis=1, tiled=True),
        lax.all_to_all(text_tags, "ctx", split_axis=1, concat_axis=1, tiled=True),
    )
    second_text, second_tags = (
        lax.all_to_all(
            jnp.take(first_text, inverse, axis=1), "ctx", split_axis=1, concat_axis=1, tiled=True
        ),
        lax.all_to_all(
            jnp.take(first_tags, inverse, axis=1), "ctx", split_axis=1, concat_axis=1, tiled=True
        ),
    )
    visiting = second_text.reshape(2, text_rows, feature_width)
    visiting_tags = second_tags.reshape(text_rows, frame_blocks + 1).astype(jnp.int32)
    grad_visit, home_adjoint = attend(
        visiting[0],
        visiting[1],
        frame_kv[0],
        frame_kv[1],
        visiting_tags[:, 1:],
        visiting_tags[:, 0],
        frame_seg,
        sink_logit,
    )
    returning = lax.all_to_all(
        grad_visit.reshape(1, owners, text_rows // owners, feature_width),
        "ctx",
        split_axis=1,
        concat_axis=1,
        tiled=True,
    )
    grad_query = lax.all_to_all(
        jnp.take(returning, pairing, axis=1), "ctx", split_axis=1, concat_axis=1, tiled=True
    ).reshape(text_rows, feature_width)
    grad_kv = lax.all_to_all(home_adjoint, "head", split_axis=1, concat_axis=2, tiled=True)
    return (grad_query, grad_kv)


def solution(mesh):
    in_specs = (
        P("ctx", "head"),
        P("ctx", "head"),
        P(None, "ctx", "head"),
        P("head"),
        P(),
        P("ctx", None),
        P("ctx"),
        P("ctx"),
    )
    out_specs = (P("ctx", "head"), P(None, ("ctx", "head"), None))
    return jax.shard_map(shards, mesh=mesh, in_specs=in_specs, out_specs=out_specs, check_vma=False)
```

profile of v0, /device:TPU:1, one launch (start us, length us, event | category | flops | bytes accessed | tf_op | source)
XLA Modules:
  0.0 181.7 jit_solution(7947610529917276390)
XLA Ops:
  3.0 20.8 %all-to-all-start = ((bf16[1,128,1,5]{3,2,0,1:T(2,128)(2,1)}), bf16[1,128,1,5]{3,2,0,1:T(2,128)(2,1)S(1)}, u32[]{:S(2)}, u32[]{:S(2)}) async-start(bf16[1,128,1,5]{3,2,0,1:T(2,128)(2,1)} %copy.78), calls=%async_computation | async-start | bytes 131072 | tf_op jit(solution)/shard_map/all_to_all | solution.py:66
  26.7 10.0 %all-to-all-done = bf16[1,128,1,5]{3,2,0,1:T(2,128)(2,1)S(1)} async-done(((bf16[1,128,1,5]{3,2,0,1:T(2,128)(2,1)}), bf16[1,128,1,5]{3,2,0,1:T(2,128)(2,1)S(1)}, u32[]{:S(2)}, u32[]{:S(2)}) %all-to-all-start) | async-done | bytes 1312 | tf_op jit(solution)/shard_map/all_to_all | solution.py:66
  36.8 6.2 %all-to-all-start.2 = ((bf16[2,128,1,640]{3,0,2,1:T(2,128)(2,1)}), bf16[2,128,1,640]{3,0,2,1:T(2,128)(2,1)S(1)}, u32[]{:S(2)}, u32[]{:S(2)}) async-start(bf16[2,128,1,640]{3,0,2,1:T(2,128)(2,1)} %copy.82), calls=%async_computation.2 | async-start | bytes 655360 | tf_op jit(solution)/shard_map/all_to_all | solution.py:65
  44.6 13.1 %all-to-all-done.2 = bf16[2,128,1,640]{3,0,2,1:T(2,128)(2,1)S(1)} async-done(((bf16[2,128,1,640]{3,0,2,1:T(2,128)(2,1)}), bf16[2,128,1,640]{3,0,2,1:T(2,128)(2,1)S(1)}, u32[]{:S(2)}, u32[]{:S(2)}) %all-to-all-start.2) | async-done | bytes 327712 | tf_op jit(solution)/shard_map/all_to_all | solution.py:65
  57.7 8.6 %all-to-all-start.1 = ((bf16[1,128,1,5]{3,2,0,1:T(2,128)(2,1)}), bf16[1,128,1,5]{3,2,0,1:T(2,128)(2,1)S(1)}, u32[]{:S(2)}, u32[]{:S(2)}) async-start(bf16[1,128,1,5]{3,2,0,1:T(2,128)(2,1)} %copy.81), calls=%async_computation.1 | async-start | bytes 131072 | tf_op jit(solution)/shard_map/all_to_all | solution.py:72
  66.3 1.3 gather_fusion.1
  68.7 10.5 %all-to-all-done.1 = bf16[1,128,1,5]{3,2,0,1:T(2,128)(2,1)S(1)} async-done(((bf16[1,128,1,5]{3,2,0,1:T(2,128)(2,1)}), bf16[1,128,1,5]{3,2,0,1:T(2,128)(2,1)S(1)}, u32[]{:S(2)}, u32[]{:S(2)}) %all-to-all-start.1) | async-done | bytes 1312 | tf_op jit(solution)/shard_map/all_to_all | solution.py:72
  79.2 6.4 %all-to-all-start.3 = ((bf16[2,128,1,640]{3,0,2,1:T(2,128)(2,1)}), bf16[2,128,1,640]{3,0,2,1:T(2,128)(2,1)S(1)}, u32[]{:S(2)}, u32[]{:S(2)}) async-start(bf16[2,128,1,640]{3,0,2,1:T(2,128)(2,1)} %fusion.11), calls=%async_computation.3 | async-start | bytes 655360 | tf_op jit(solution)/shard_map/all_to_all | solution.py:69
  86.7 13.5 %all-to-all-done.3 = bf16[2,128,1,640]{3,0,2,1:T(2,128)(2,1)S(1)} async-done(((bf16[2,128,1,640]{3,0,2,1:T(2,128)(2,1)}), bf16[2,128,1,640]{3,0,2,1:T(2,128)(2,1)S(1)}, u32[]{:S(2)}, u32[]{:S(2)}) %all-to-all-start.3) | async-done | bytes 327712 | tf_op jit(solution)/shard_map/all_to_all | solution.py:69
  102.8 1.5 fusion.2
  105.5 1.6 reduce.2
  107.9 8.0 %all-to-all-start.4 = ((bf16[128,2,320]{2,1,0:T(2,128)(2,1)}), bf16[128,2,320]{2,1,0:T(2,128)(2,1)S(1)}, u32[]{:S(2)}, u32[]{:S(2)}) async-start(bf16[128,2,320]{2,1,0:T(2,128)(2,1)} %reshape.298), calls=%async_computation.4 | async-start | bytes 393216 | tf_op jit(solution)/shard_map/all_to_all | solution.py:88
  115.9 1.4 convolution_convert_fusion
  117.4 12.5 %all-to-all-done.4 = bf16[128,2,320]{2,1,0:T(2,128)(2,1)S(1)} async-done(((bf16[128,2,320]{2,1,0:T(2,128)(2,1)}), bf16[128,2,320]{2,1,0:T(2,128)(2,1)S(1)}, u32[]{:S(2)}, u32[]{:S(2)}) %all-to-all-start.4) | async-done | bytes 163872 | tf_op jit(solution)/shard_map/all_to_all | solution.py:88
  131.4 1.6 reduce.3
  133.9 7.4 %all-to-all-start.5 = ((bf16[128,2,320]{2,1,0:T(2,128)(2,1)}), bf16[128,2,320]{2,1,0:T(2,128)(2,1)}, u32[]{:S(2)}, u32[]{:S(2)}) async-start(bf16[128,2,320]{2,1,0:T(2,128)(2,1)} %reshape.300), calls=%async_computation.5 | async-start | bytes 393216 | tf_op jit(solution)/shard_map/all_to_all | solution.py:95
  141.7 1.1 copy.95
  142.8 1.1 copy.94
  144.0 4.0 %pad_maximum_fusion = bf16[2,512,640]{2,0,1:T(2,128)(2,1)} fusion(bf16[1,512,640]{2,0,1:T(2,128)(2,1)S(1)} %copy.95, bf16[1,512,640]{2,0,1:T(2,128)(2,1)S(1)} %copy.94), kind=kLoop, calls=%fused_computation.11 | loop fusion | flops 2621440 | bytes 2621440 | tf_op jit(solution)/shard_map/stack | solution.py:47
  148.0 6.6 %all-to-all-done.5 = bf16[128,2,320]{2,1,0:T(2,128)(2,1)} async-done(((bf16[128,2,320]{2,1,0:T(2,128)(2,1)}), bf16[128,2,320]{2,1,0:T(2,128)(2,1)}, u32[]{:S(2)}, u32[]{:S(2)}) %all-to-all-start.5) | async-done | bytes 163872 | tf_op jit(solution)/shard_map/all_to_all | solution.py:95
  154.6 8.3 %all-to-all-start.6 = ((bf16[2,512,640]{2,0,1:T(2,128)(2,1)}), bf16[2,512,640]{2,0,1:T(2,128)(2,1)S(1)}, u32[]{:S(2)}, u32[]{:S(2)}) async-start(bf16[2,512,640]{2,0,1:T(2,128)(2,1)} %pad_maximum_fusion), calls=%async_computation.6 | async-start | bytes 2621440 | tf_op jit(solution)/shard_map/all_to_all | solution.py:98
  162.9 1.6 reshape.301
  165.3 14.1 %all-to-all-done.6 = bf16[2,512,640]{2,0,1:T(2,128)(2,1)S(1)} async-done(((bf16[2,512,640]{2,0,1:T(2,128)(2,1)}), bf16[2,512,640]{2,0,1:T(2,128)(2,1)S(1)}, u32[]{:S(2)}, u32[]{:S(2)}) %all-to-all-start.6) | async-done | bytes 1310752 | tf_op jit(solution)/shard_map/all_to_all | solution.py:98
  180.4 1.4 all_to_all.40
  (62 shorter events, 18.1 us)
Async XLA Ops:
  0.6 42.3 %copy-start.6 = (s32[128]{0:T(128)S(1)}, s32[128]{0:T(128)}, u32[]{:S(2)}) copy-start(s32[128]{0:T(128)} %param.12) | copy-start | bytes 1540
  0.6 42.3 %copy-start = (bf16[2,512,640]{2,1,0:T(8,128)(2,1)S(1)}, bf16[2,512,640]{2,1,0:T(8,128)(2,1)}, u32[]{:S(2)}) copy-start(bf16[2,512,640]{2,1,0:T(8,128)(2,1)} %param.10) | copy-start | bytes 3932164
  3.0 33.8 %all-to-all-start = ((bf16[1,128,1,5]{3,2,0,1:T(2,128)(2,1)}), bf16[1,128,1,5]{3,2,0,1:T(2,128)(2,1)S(1)}, u32[]{:S(2)}, u32[]{:S(2)}) async-start(bf16[1,128,1,5]{3,2,0,1:T(2,128)(2,1)} %copy.78), calls=%async_computation | async-start | bytes 131072 | tf_op jit(solution)/shard_map/all_to_all | solution.py:66
  36.8 20.9 %all-to-all-start.2 = ((bf16[2,128,1,640]{3,0,2,1:T(2,128)(2,1)}), bf16[2,128,1,640]{3,0,2,1:T(2,128)(2,1)S(1)}, u32[]{:S(2)}, u32[]{:S(2)}) async-start(bf16[2,128,1,640]{3,0,2,1:T(2,128)(2,1)} %copy.82), calls=%async_computation.2 | async-start | bytes 655360 | tf_op jit(solution)/shard_map/all_to_all | solution.py:65
  57.7 21.5 %all-to-all-start.1 = ((bf16[1,128,1,5]{3,2,0,1:T(2,128)(2,1)}), bf16[1,128,1,5]{3,2,0,1:T(2,128)(2,1)S(1)}, u32[]{:S(2)}, u32[]{:S(2)}) async-start(bf16[1,128,1,5]{3,2,0,1:T(2,128)(2,1)} %copy.81), calls=%async_computation.1 | async-start | bytes 131072 | tf_op jit(solution)/shard_map/all_to_all | solution.py:72
  79.2 21.0 %all-to-all-start.3 = ((bf16[2,128,1,640]{3,0,2,1:T(2,128)(2,1)}), bf16[2,128,1,640]{3,0,2,1:T(2,128)(2,1)S(1)}, u32[]{:S(2)}, u32[]{:S(2)}) async-start(bf16[2,128,1,640]{3,0,2,1:T(2,128)(2,1)} %fusion.11), calls=%async_computation.3 | async-start | bytes 655360 | tf_op jit(solution)/shard_map/all_to_all | solution.py:69
  85.6 1.0 copy-start.4
  100.9 0.7 copy-start.5
  101.1 1.1 copy-start.2
  104.3 11.6 %copy-start.3 = (bf16[1,128,1,640]{1,3,2,0:T(8,128)(2,1)S(1)}, bf16[1,128,1,640]{1,3,2,0:T(8,128)(2,1)}, u32[]{:S(2)}) copy-start(bf16[1,128,1,640]{1,3,2,0:T(8,128)(2,1)} %copy-done.2) | copy-start | bytes 491524
  107.9 21.9 %all-to-all-start.4 = ((bf16[128,2,320]{2,1,0:T(2,128)(2,1)}), bf16[128,2,320]{2,1,0:T(2,128)(2,1)S(1)}, u32[]{:S(2)}, u32[]{:S(2)}) async-start(bf16[128,2,320]{2,1,0:T(2,128)(2,1)} %reshape.298), calls=%async_computation.4 | async-start | bytes 393216 | tf_op jit(solution)/shard_map/all_to_all | solution.py:88
  131.4 10.2 %copy-start.1 = (bf16[5,128,512]{2,1,0:T(8,128)(2,1)S(1)}, bf16[5,128,512]{2,1,0:T(8,128)(2,1)}, u32[]{:S(2)}) copy-start(bf16[5,128,512]{2,1,0:T(8,128)(2,1)} %convolution_convert_fusion) | copy-start | bytes 1966084
  133.9 20.7 %all-to-all-start.5 = ((bf16[128,2,320]{2,1,0:T(2,128)(2,1)}), bf16[128,2,320]{2,1,0:T(2,128)(2,1)}, u32[]{:S(2)}, u32[]{:S(2)}) async-start(bf16[128,2,320]{2,1,0:T(2,128)(2,1)} %reshape.300), calls=%async_computation.5 | async-start | bytes 393216 | tf_op jit(solution)/shard_map/all_to_all | solution.py:95
  154.6 24.7 %all-to-all-start.6 = ((bf16[2,512,640]{2,0,1:T(2,128)(2,1)}), bf16[2,512,640]{2,0,1:T(2,128)(2,1)S(1)}, u32[]{:S(2)}, u32[]{:S(2)}) async-start(bf16[2,512,640]{2,0,1:T(2,128)(2,1)} %pad_maximum_fusion), calls=%async_computation.6 | async-start | bytes 2621440 | tf_op jit(solution)/shard_map/all_to_all | solution.py:98
where the time goes:
time: 182 us
  waiting for transfers between devices  80.3 us (44%)
  starting transfers between devices  65.6 us (36%)
  local copies, waits for them, and re-layouts  17.5 us (10%)
  other arithmetic  12.7 us (7%)
  matrix products  4.67 us (3%)
    all_to_all x1, starting transfers between devices, shards(): lax.all_to_all(text_tags, 'ctx', split_axis=1, concat_axis=1, tiled=True)  20.8 us
    all_to_all x1, waiting for transfers between devices, shards(): lax.all_to_all(home_adjoint, 'head', split_axis=1, concat_axis=2, tiled=T...  14.1 us
    all_to_all x1, waiting for transfers between devices, shards(): lax.all_to_all(jnp.take(first_text, inverse, axis=1), 'ctx', split_axis=1...  13.5 us
    all_to_all x1, waiting for transfers between devices, shards(): lax.all_to_all(stacked, 'ctx', split_axis=1, concat_axis=1, tiled=True)  13.1 us
    all_to_all x1, waiting for transfers between devices, shards(): lax.all_to_all(grad_visit.reshape(1, owners, text_rows // owners, feature...  12.5 us
    all_to_all x1, waiting for transfers between devices, shards(): lax.all_to_all(jnp.take(first_tags, inverse, axis=1), 'ctx', split_axis=1...  10.5 us
    all_to_all x1, waiting for transfers between devices, shards(): lax.all_to_all(text_tags, 'ctx', split_axis=1, concat_axis=1, tiled=True)  10 us
    all_to_all x1, starting transfers between devices, shards(): lax.all_to_all(jnp.take(first_tags, inverse, axis=1), 'ctx', split_axis=1...  8.58 us
  transfers between devices with their start and end apart: 7, of which 7 were waited for; matrix products, arithmetic and copies ran while one was open for 10% of the time, Pallas kernels for 0%

commit v1 on v0

--- a/solution.py
+++ b/solution.py
@@ -5,6 +5,12 @@
 
 DH = 128
 BLOCK = 128
+
+
+def exchange_blocks(x, mesh_axis, split, join):
+    parts = jnp.split(x, lax.axis_size(mesh_axis), axis=split)
+    got = lax.all_to_all(jnp.stack(parts), mesh_axis, 0, 0)
+    return jnp.concatenate(got, axis=join)
 
 
 def attend(query_rows, grad_rows, key_rows, value_rows, row_mask, text_ids, frame_ids, sink_logit):
@@ -95,7 +101,7 @@
     grad_query = lax.all_to_all(
         jnp.take(returning, pairing, axis=1), "ctx", split_axis=1, concat_axis=1, tiled=True
     ).reshape(text_rows, feature_width)
-    grad_kv = lax.all_to_all(home_adjoint, "head", split_axis=1, concat_axis=2, tiled=True)
+    grad_kv = exchange_blocks(home_adjoint, "head", 1, 2)
     return (grad_query, grad_kv)
 
 

time: 182 us -> 182 us (level)
  waiting for transfers between devices: 80.3 us -> 87.1 us
  other arithmetic: 12.7 us -> 10.2 us
  local copies, waits for them, and re-layouts: 17.5 us -> 15 us
    all_to_all x1, waiting for transfers between devices: 6.64 us -> 12.1 us  [shards(): lax.all_to_all(jnp.take(returning, pairing, axis=1), 'ctx', split_axis=1,...]
    reshape x0 -> x2, local copies, waits for them, and re-layouts: none -> 2.95 us  [exchange_blocks(): return jnp.concatenate(got, axis=join)]
    another operation x2 -> x3, other arithmetic: 4.79 us -> 2.12 us  [the longest x2 1.46 us: exchange_blocks(): got = lax.all_to_all(jnp.stack(parts), mesh_axis, 0, 0)]
    all_to_all x2 -> x0, local copies, waits for them, and re-layouts: 2.38 us -> none  [shards(): lax.all_to_all(home_adjoint, 'head', split_axis=1, concat_axis=2, tiled=T...]
    another operation x2 -> x0, local copies, waits for them, and re-layouts: 2.29 us -> none  [attend(): jnp.stack([grad_keys.reshape(frame_rows, -1), grad_values.reshape(frame_r...]
  transfers between devices with their start and end apart: 7 -> 7, of which waited for: 7 -> 7; matrix products, arithmetic and copies ran while one was open for 10% -> 7% of each run, Pallas kernels for 0% -> 0%
where the time goes in v1:
time: 182 us; the launch traced here: 181 us
  waiting for transfers between devices  87.1 us (48%)
  starting transfers between devices  64.4 us (35%)
  local copies, waits for them, and re-layouts  15 us (8%)
  other arithmetic  10.2 us (6%)
  matrix products  3.78 us (2%)
    all_to_all x1, starting transfers between devices, shards(): lax.all_to_all(text_tags, 'ctx', split_axis=1, concat_axis=1, tiled=True)  20.8 us
    all_to_all x1, waiting for transfers between devices, exchange_blocks(): got = lax.all_to_all(jnp.stack(parts), mesh_axis, 0, 0)  15.4 us
    all_to_all x1, waiting for transfers between devices, shards(): lax.all_to_all(jnp.take(first_text, inverse, axis=1), 'ctx', split_axis=1...  13.5 us
    all_to_all x1, waiting for transfers between devices, shards(): lax.all_to_all(stacked, 'ctx', split_axis=1, concat_axis=1, tiled=True)  13.1 us
    all_to_all x1, waiting for transfers between devices, shards(): lax.all_to_all(grad_visit.reshape(1, owners, text_rows // owners, feature...  12.5 us
    all_to_all x1, waiting for transfers between devices, shards(): lax.all_to_all(jnp.take(returning, pairing, axis=1), 'ctx', split_axis=1,...  12.1 us
    all_to_all x1, waiting for transfers between devices, shards(): lax.all_to_all(jnp.take(first_tags, inverse, axis=1), 'ctx', split_axis=1...  10.5 us
    all_to_all x1, waiting for transfers between devices, shards(): lax.all_to_all(text_tags, 'ctx', split_axis=1, concat_axis=1, tiled=True)  10 us
  transfers between devices with their start and end apart: 7, of which 7 were waited for; matrix products, arithmetic and copies ran while one was open for 7% of the time, Pallas kernels for 0%

profile of v1, /device:TPU:1, one launch (start us, length us, event | category | flops | bytes accessed | tf_op | source)
XLA Modules:
  0.0 181.4 jit_solution(14637316252824624414)
XLA Ops:
  3.0 20.8 %all-to-all-start = ((bf16[1,128,1,5]{3,2,0,1:T(2,128)(2,1)}), bf16[1,128,1,5]{3,2,0,1:T(2,128)(2,1)S(1)}, u32[]{:S(2)}, u32[]{:S(2)}) async-start(bf16[1,128,1,5]{3,2,0,1:T(2,128)(2,1)} %copy.74), calls=%async_computation | async-start | bytes 131072 | tf_op jit(solution)/shard_map/all_to_all | solution.py:72
  24.6 1.0 maximum_bitcast_fusion
  25.6 1.1 copy.78
  26.7 10.0 %all-to-all-done = bf16[1,128,1,5]{3,2,0,1:T(2,128)(2,1)S(1)} async-done(((bf16[1,128,1,5]{3,2,0,1:T(2,128)(2,1)}), bf16[1,128,1,5]{3,2,0,1:T(2,128)(2,1)S(1)}, u32[]{:S(2)}, u32[]{:S(2)}) %all-to-all-start) | async-done | bytes 1312 | tf_op jit(solution)/shard_map/all_to_all | solution.py:72
  36.8 6.2 %all-to-all-start.2 = ((bf16[2,128,1,640]{3,0,2,1:T(2,128)(2,1)}), bf16[2,128,1,640]{3,0,2,1:T(2,128)(2,1)S(1)}, u32[]{:S(2)}, u32[]{:S(2)}) async-start(bf16[2,128,1,640]{3,0,2,1:T(2,128)(2,1)} %copy.78), calls=%async_computation.2 | async-start | bytes 655360 | tf_op jit(solution)/shard_map/all_to_all | solution.py:71
  44.6 13.1 %all-to-all-done.2 = bf16[2,128,1,640]{3,0,2,1:T(2,128)(2,1)S(1)} async-done(((bf16[2,128,1,640]{3,0,2,1:T(2,128)(2,1)}), bf16[2,128,1,640]{3,0,2,1:T(2,128)(2,1)S(1)}, u32[]{:S(2)}, u32[]{:S(2)}) %all-to-all-start.2) | async-done | bytes 327712 | tf_op jit(solution)/shard_map/all_to_all | solution.py:71
  57.7 8.6 %all-to-all-start.1 = ((bf16[1,128,1,5]{3,2,0,1:T(2,128)(2,1)}), bf16[1,128,1,5]{3,2,0,1:T(2,128)(2,1)S(1)}, u32[]{:S(2)}, u32[]{:S(2)}) async-start(bf16[1,128,1,5]{3,2,0,1:T(2,128)(2,1)} %copy.77), calls=%async_computation.1 | async-start | bytes 131072 | tf_op jit(solution)/shard_map/all_to_all | solution.py:78
  66.3 1.3 gather_fusion.1
  67.5 1.1 fusion.18
  68.7 10.5 %all-to-all-done.1 = bf16[1,128,1,5]{3,2,0,1:T(2,128)(2,1)S(1)} async-done(((bf16[1,128,1,5]{3,2,0,1:T(2,128)(2,1)}), bf16[1,128,1,5]{3,2,0,1:T(2,128)(2,1)S(1)}, u32[]{:S(2)}, u32[]{:S(2)}) %all-to-all-start.1) | async-done | bytes 1312 | tf_op jit(solution)/shard_map/all_to_all | solution.py:78
  79.2 6.4 %all-to-all-start.3 = ((bf16[2,128,1,640]{3,0,2,1:T(2,128)(2,1)}), bf16[2,128,1,640]{3,0,2,1:T(2,128)(2,1)S(1)}, u32[]{:S(2)}, u32[]{:S(2)}) async-start(bf16[2,128,1,640]{3,0,2,1:T(2,128)(2,1)} %fusion.18), calls=%async_computation.3 | async-start | bytes 655360 | tf_op jit(solution)/shard_map/all_to_all | solution.py:75
  86.7 13.5 %all-to-all-done.3 = bf16[2,128,1,640]{3,0,2,1:T(2,128)(2,1)S(1)} async-done(((bf16[2,128,1,640]{3,0,2,1:T(2,128)(2,1)}), bf16[2,128,1,640]{3,0,2,1:T(2,128)(2,1)S(1)}, u32[]{:S(2)}, u32[]{:S(2)}) %all-to-all-start.3) | async-done | bytes 327712 | tf_op jit(solution)/shard_map/all_to_all | solution.py:75
  105.2 1.6 reduce.2
  107.6 8.0 %all-to-all-start.4 = ((bf16[128,2,320]{2,1,0:T(2,128)(2,1)}), bf16[128,2,320]{2,1,0:T(2,128)(2,1)S(1)}, u32[]{:S(2)}, u32[]{:S(2)}) async-start(bf16[128,2,320]{2,1,0:T(2,128)(2,1)} %reshape.306), calls=%async_computation.4 | async-start | bytes 393216 | tf_op jit(solution)/shard_map/all_to_all | solution.py:94
  115.6 1.4 convolution_convert_fusion
  117.1 12.5 %all-to-all-done.4 = bf16[128,2,320]{2,1,0:T(2,128)(2,1)S(1)} async-done(((bf16[128,2,320]{2,1,0:T(2,128)(2,1)}), bf16[128,2,320]{2,1,0:T(2,128)(2,1)S(1)}, u32[]{:S(2)}, u32[]{:S(2)}) %all-to-all-start.4) | async-done | bytes 163872 | tf_op jit(solution)/shard_map/all_to_all | solution.py:94
  131.1 1.7 reduce.3
  133.7 6.2 %all-to-all-start.5 = ((bf16[128,2,320]{2,1,0:T(2,128)(2,1)}), bf16[128,2,320]{2,1,0:T(2,128)(2,1)S(1)}, u32[]{:S(2)}, u32[]{:S(2)}) async-start(bf16[128,2,320]{2,1,0:T(2,128)(2,1)} %reshape.308), calls=%async_computation.5 | async-start | bytes 393216 | tf_op jit(solution)/shard_map/all_to_all | solution.py:101
  140.4 1.2 pad_maximum_fusion
  141.6 12.1 %all-to-all-done.5 = bf16[128,2,320]{2,1,0:T(2,128)(2,1)S(1)} async-done(((bf16[128,2,320]{2,1,0:T(2,128)(2,1)}), bf16[128,2,320]{2,1,0:T(2,128)(2,1)S(1)}, u32[]{:S(2)}, u32[]{:S(2)}) %all-to-all-start.5) | async-done | bytes 163872 | tf_op jit(solution)/shard_map/all_to_all | solution.py:101
  153.7 8.4 %all-to-all-start.6 = ((bf16[4,2,128,640]{2,3,1,0:T(8,128)(2,1)}), bf16[4,2,128,640]{2,3,1,0:T(8,128)(2,1)S(1)}, u32[]{:S(2)}, u32[]{:S(2)}) async-start(bf16[4,2,128,640]{2,3,1,0:T(8,128)(2,1)} %pad_maximum_fusion), calls=%async_computation.6 | async-start | bytes 2621440 | tf_op jit(solution)/shard_map/all_to_all | solution.py:12
  163.0 15.4 %all-to-all-done.6 = bf16[4,2,128,640]{2,3,1,0:T(8,128)(2,1)S(1)} async-done(((bf16[4,2,128,640]{2,3,1,0:T(8,128)(2,1)}), bf16[4,2,128,640]{2,3,1,0:T(8,128)(2,1)S(1)}, u32[]{:S(2)}, u32[]{:S(2)}) %all-to-all-start.6) | async-done | bytes 1310752 | tf_op jit(solution)/shard_map/all_to_all | solution.py:12
  178.5 1.6 copy.90
  180.1 1.4 reshape.262
  (61 shorter events, 15.6 us)
Async XLA Ops:
  0.6 42.3 %copy-start.6 = (s32[128]{0:T(128)S(1)}, s32[128]{0:T(128)}, u32[]{:S(2)}) copy-start(s32[128]{0:T(128)} %param.12) | copy-start | bytes 1540
  0.6 42.3 %copy-start = (bf16[2,512,640]{2,1,0:T(8,128)(2,1)S(1)}, bf16[2,512,640]{2,1,0:T(8,128)(2,1)}, u32[]{:S(2)}) copy-start(bf16[2,512,640]{2,1,0:T(8,128)(2,1)} %param.10) | copy-start | bytes 3932164
  3.0 33.8 %all-to-all-start = ((bf16[1,128,1,5]{3,2,0,1:T(2,128)(2,1)}), bf16[1,128,1,5]{3,2,0,1:T(2,128)(2,1)S(1)}, u32[]{:S(2)}, u32[]{:S(2)}) async-start(bf16[1,128,1,5]{3,2,0,1:T(2,128)(2,1)} %copy.74), calls=%async_computation | async-start | bytes 131072 | tf_op jit(solution)/shard_map/all_to_all | solution.py:72
  36.8 20.9 %all-to-all-start.2 = ((bf16[2,128,1,640]{3,0,2,1:T(2,128)(2,1)}), bf16[2,128,1,640]{3,0,2,1:T(2,128)(2,1)S(1)}, u32[]{:S(2)}, u32[]{:S(2)}) async-start(bf16[2,128,1,640]{3,0,2,1:T(2,128)(2,1)} %copy.78), calls=%async_computation.2 | async-start | bytes 655360 | tf_op jit(solution)/shard_map/all_to_all | solution.py:71
  57.7 21.5 %all-to-all-start.1 = ((bf16[1,128,1,5]{3,2,0,1:T(2,128)(2,1)}), bf16[1,128,1,5]{3,2,0,1:T(2,128)(2,1)S(1)}, u32[]{:S(2)}, u32[]{:S(2)}) async-start(bf16[1,128,1,5]{3,2,0,1:T(2,128)(2,1)} %copy.77), calls=%async_computation.1 | async-start | bytes 131072 | tf_op jit(solution)/shard_map/all_to_all | solution.py:78
  79.2 21.0 %all-to-all-start.3 = ((bf16[2,128,1,640]{3,0,2,1:T(2,128)(2,1)}), bf16[2,128,1,640]{3,0,2,1:T(2,128)(2,1)S(1)}, u32[]{:S(2)}, u32[]{:S(2)}) async-start(bf16[2,128,1,640]{3,0,2,1:T(2,128)(2,1)} %fusion.18), calls=%async_computation.3 | async-start | bytes 655360 | tf_op jit(solution)/shard_map/all_to_all | solution.py:75
  85.6 1.0 copy-start.4
  101.5 0.7 copy-start.5
  101.7 1.1 copy-start.2
  104.0 11.6 %copy-start.3 = (bf16[1,128,1,640]{1,3,2,0:T(8,128)(2,1)S(1)}, bf16[1,128,1,640]{1,3,2,0:T(8,128)(2,1)}, u32[]{:S(2)}) copy-start(bf16[1,128,1,640]{1,3,2,0:T(8,128)(2,1)} %copy.100) | copy-start | bytes 491524
  107.6 21.9 %all-to-all-start.4 = ((bf16[128,2,320]{2,1,0:T(2,128)(2,1)}), bf16[128,2,320]{2,1,0:T(2,128)(2,1)S(1)}, u32[]{:S(2)}, u32[]{:S(2)}) async-start(bf16[128,2,320]{2,1,0:T(2,128)(2,1)} %reshape.306), calls=%async_computation.4 | async-start | bytes 393216 | tf_op jit(solution)/shard_map/all_to_all | solution.py:94
  131.1 9.0 %copy-start.1 = (bf16[5,128,512]{2,1,0:T(8,128)(2,1)S(1)}, bf16[5,128,512]{2,1,0:T(8,128)(2,1)}, u32[]{:S(2)}) copy-start(bf16[5,128,512]{2,1,0:T(8,128)(2,1)} %convolution_convert_fusion) | copy-start | bytes 1966084
  133.7 20.1 %all-to-all-start.5 = ((bf16[128,2,320]{2,1,0:T(2,128)(2,1)}), bf16[128,2,320]{2,1,0:T(2,128)(2,1)S(1)}, u32[]{:S(2)}, u32[]{:S(2)}) async-start(bf16[128,2,320]{2,1,0:T(2,128)(2,1)} %reshape.308), calls=%async_computation.5 | async-start | bytes 393216 | tf_op jit(solution)/shard_map/all_to_all | solution.py:101
  153.7 24.8 %all-to-all-start.6 = ((bf16[4,2,128,640]{2,3,1,0:T(8,128)(2,1)}), bf16[4,2,128,640]{2,3,1,0:T(8,128)(2,1)S(1)}, u32[]{:S(2)}, u32[]{:S(2)}) async-start(bf16[4,2,128,640]{2,3,1,0:T(8,128)(2,1)} %pad_maximum_fusion), calls=%async_computation.6 | async-start | bytes 2621440 | tf_op jit(solution)/shard_map/all_to_all | solution.py:12
